TPU v7x, 128 devices: a whole 4x4x4 slice. The times are simulated.
128 devices in a mesh: seq: 16 (over z, y_hi, core), grp: 8 (over x, y_lo).
Axes of the slice: x: 4, y: 4 (y_hi: 2, y_lo: 2; y = y_hi * 2 + y_lo), z: 4, core: 2. Of those that a mesh axis runs over, the one named last changes fastest.
Arguments:
- tokens: bfloat16 [262144, 1280], P(('seq', 'grp')), may hold values from -27 to 27
- slot_keys: bfloat16 [1280, 512], replicated, may hold values from -1.5 to 1.5
- norm_gain: float32 [128, 1280], P(('seq', 'grp')), may hold values from 0.1 to 1.9
- w_in: bfloat16 [128, 1280, 2560], P(('seq', 'grp')), may hold values from -0.15625 to 0.15625
- w_out: bfloat16 [128, 2560, 1280], P(('seq', 'grp')), may hold values from -0.125 to 0.125
Outputs:
- mixed: bfloat16 [262144, 1280], P(('seq', 'grp'))
All inputs are finite; a program needn't handle non-finite values.
Results may differ from a plain program's by a relative error of at most 0.007.
Values may be sent and summed in bfloat16 or wider, within the bound.
A program may use at most 128 MiB of HBM per device.

v0:
```python
import jax
import jax.numpy as jnp
from jax import lax
from jax.sharding import PartitionSpec as P


def in_one_piece(arrays, axis, split_dim, concat_dim, along):
    columns = [a.reshape(*a.shape[:along], -1) for a in arrays]
    both = jnp.concatenate(columns, axis=along)
    out, at, finished = (
        lax.all_to_all(both, axis, split_axis=split_dim, concat_axis=concat_dim, tiled=True),
        0,
        [],
    )
    for a, column in zip(arrays, columns):
        piece = out[..., at : at + column.shape[along]]
        finished.append(piece.reshape(*piece.shape[:along], *a.shape[along:]))
        at += column.shape[along]
    return tuple(finished)


def on_device(tokens, slot_keys, norm_gain, w_in, w_out):
    devices = lax.axis_size(("seq", "grp"))
    logits = jnp.dot(tokens, slot_keys, preferred_element_type=jnp.float32)
    per_dev = logits.shape[1] // devices
    maxima = jnp.max(logits, axis=0)
    scores = jnp.exp(logits - maxima[None, :])
    totals = jnp.sum(scores, axis=0)
    weights = scores.astype(jnp.bfloat16)
    dims = (((0,), (0,)), ((), ()))
    numer_local = lax.dot_general(weights, tokens, dims, preferred_element_type=jnp.float32)
    parts, peaks, sums = in_one_piece((numer_local, maxima, totals), ("seq", "grp"), 0, 0, 1)
    peaks = peaks.reshape(devices, per_dev)
    factor = jnp.exp(peaks - jnp.max(peaks, axis=0, keepdims=True))
    numer = jnp.sum(parts.reshape(devices, per_dev, -1) * factor[:, :, None], axis=0)
    own_total = jnp.sum(sums.reshape(devices, per_dev) * factor, axis=0)
    slot_in = numer / own_total[:, None]
    normed = (slot_in * norm_gain[0][None, :]).astype(jnp.bfloat16)
    hidden = jax.nn.gelu(jnp.dot(normed, w_in[0], preferred_element_type=jnp.float32)).astype(
        jnp.bfloat16
    )
    expert_out = jnp.dot(hidden, w_out[0], preferred_element_type=jnp.float32).astype(jnp.bfloat16)
    row_top = jnp.max(logits, axis=1, keepdims=True)
    row_exp = jnp.exp(logits - row_top)
    combine = (row_exp / jnp.sum(row_exp, axis=1, keepdims=True)).astype(jnp.bfloat16)
    gathered = lax.all_gather(expert_out, ("seq", "grp"), axis=0, tiled=True)
    mixed = jnp.dot(combine, gathered, preferred_element_type=jnp.float32)
    return mixed.astype(jnp.bfloat16)


def solution(mesh):
    return jax.shard_map(
        on_device,
        mesh=mesh,
        in_specs=(
            P(("seq", "grp"), None),
            P(),
            P(("seq", "grp"), None),
            P(("seq", "grp"), None, None),
            P(("seq", "grp"), None, None),
        ),
        out_specs=P(("seq", "grp"), None),
        check_vma=False,
    )
```

profile of v0, /device:TPU:1, one launch (start us, length us, event | category | flops | bytes accessed | tf_op | source)
XLA Modules:
  0.0 423.7 jit_solution(511834206281356095)
XLA Ops:
  6.5 0.0 copy-start
  6.5 1.3 copy-done
  7.9 7.1 %fusion.44 = (f32[2048]{0:T(1024)S(1)}, f32[512]{0:T(512)S(1)}, f32[2048,512]{1,0:T(8,128)}) fusion(bf16[2048,1280]{1,0:T(8,128)(2,1)} %param.5, bf16[1280,512]{1,0:T(8,128)(2,1)S(1)} %copy-done), kind=kOutput, calls=%fused_computation.42 | convolution fusion | flops 2686449152 | bytes 10758144 | tf_op jit(solution)/shard_map/dot_general | solution.py:24
  14.9 0.3 concatenate.14
  15.3 0.0 copy-start.1
  15.3 8.4 %fusion.13 = f32[512,1280]{1,0:T(8,128)} fusion(bf16[2048,1280]{1,0:T(8,128)(2,1)} %param.5, f32[2048,512]{1,0:T(8,128)} %get-tuple-element.13, f32[512]{0:T(512)S(1)} %get-tuple-element.8), kind=kOutput, calls=%fused_computation.14 | convolution fusion | flops 2686451712 | bytes 12060672 | tf_op jit(solution)/shard_map/dot_general | solution.py:31
  23.6 0.0 copy-done.1
  23.6 1.6 fusion.4
  25.2 0.3 concatenate.15
  25.6 3.9 concatenate.10
  29.5 5.6 %concatenate.13 = f32[128,4,1282]{2,1,0:T(4,128)} concatenate(f32[128,4,1280]{2,1,0:T(4,128)} %concatenate.10, f32[128,4,1]{2,1,0:T(4,128)S(1)} %concatenate.14, f32[128,4,1]{2,1,0:T(4,128)S(1)} %concatenate.15), dimensions={2} | concatenate | bytes 5251072 | tf_op jit(solution)/shard_map/concatenate | solution.py:9
  35.1 0.0 copy-start.2
  35.1 11.9 %all-to-all-start = ((f32[128,4,1282]{2,1,0:T(4,128)}), f32[128,4,1282]{2,1,0:T(4,128)}, u32[]{:S(2)}, u32[]{:S(2)}) async-start(f32[128,4,1282]{2,1,0:T(4,128)} %concatenate.13), calls=%async_computation | async-start | bytes 5767168 | tf_op jit(solution)/shard_map/all_to_all | solution.py:11
  47.0 0.2 all-gather.3.cloned.1.call-start
  47.2 0.0 copy-done.2
  47.3 37.5 %all-to-all-done = f32[128,4,1282]{2,1,0:T(4,128)} async-done(((f32[128,4,1282]{2,1,0:T(4,128)}), f32[128,4,1282]{2,1,0:T(4,128)}, u32[]{:S(2)}, u32[]{:S(2)}) %all-to-all-start) | async-done | bytes 2625568 | tf_op jit(solution)/shard_map/all_to_all | solution.py:11
  84.8 4.4 %all_to_all.7 = f32[512,1282]{1,0:T(8,128)} reshape(f32[128,4,1282]{2,1,0:T(4,128)} %all-to-all-done) | data formatting | bytes 5251072 | tf_op jit(solution)/shard_map/all_to_all | solution.py:11
  89.2 1.3 slice_reduce_fusion
  90.5 3.4 slice.12
  93.9 3.9 reshape.37
  97.8 0.1 reshape_reshape.7
  97.9 0.1 reshape_reshape.6
  98.1 2.3 multiply_reduce_fusion
  100.5 7.3 %fusion.10 = bf16[1,4,1280]{2,1,0:T(4,128)(2,1)} fusion(bf16[1,2560,1280]{2,1,0:T(8,128)(2,1)} %param.9, bf16[1,1280,2560]{2,1,0:T(8,128)(2,1)} %param.8, f32[4,1280]{1,0:T(4,128)S(1)} %multiply_reduce_fusion, f32[1280]{0:T(1024)S(1)} %reduce.2, f32[4]{0:T(128)S(1)} %get-tuple-element.11), kind=kOutput, calls=%fused_computation.13 | convolution fusion | flops 52541440 | bytes 13143056 | tf_op jit(solution)/shard_map/dot_general | solution.py:42
  107.8 0.0 all-gather.3.cloned.1.call-update
  107.8 298.9 %all-gather.3.cloned.1.call-done = bf16[128,4,1280]{2,1,0:T(4,128)(2,1)} async-done(((bf16[1,4,1280]{2,1,0:T(4,128)(2,1)}), bf16[128,4,1280]{2,1,0:T(4,128)(2,1)}) %all-gather.3.cloned.1.call-update) | async-done | bytes 1310736 | tf_op jit(solution)/shard_map/all_gather | solution.py:46
  406.7 2.5 reshape.39
  409.2 7.7 %convolution_convert_fusion = bf16[2048,1280]{1,0:T(8,128)(2,1)} fusion(bf16[512,1280]{1,0:T(8,128)(2,1)S(1)} %reshape.39, f32[2048,512]{1,0:T(8,128)} %get-tuple-element.13, f32[2048]{0:T(1024)S(1)} %get-tuple-element.5, f32[2048]{0:T(1024)S(1)} %get-tuple-element.7), kind=kOutput, calls=%fused_computation | convolution fusion | flops 2690121728 | bytes 10764288 | tf_op jit(solution)/shard_map/dot_general | solution.py:47
  (3 shorter events, 0.1 us)
Async XLA Ops:
  6.5 1.3 copy-start
  15.3 8.4 %copy-start.1 = (f32[2048,512]{1,0:T(8,128)S(1)}, f32[2048,512]{1,0:T(8,128)}, u32[]{:S(2)}) copy-start(f32[2048,512]{1,0:T(8,128)} %get-tuple-element.13) | copy-start | bytes 12582916
  35.1 12.1 %copy-start.2 = (f32[1,1280]{1,0:T(1,128)S(1)}, f32[1,1280]{1,0:T(1,128)}, u32[]{:S(2)}) copy-start(f32[1,1280]{1,0:T(1,128)} %param.7) | copy-start | bytes 15364
  35.1 49.7 %all-to-all-start = ((f32[128,4,1282]{2,1,0:T(4,128)}), f32[128,4,1282]{2,1,0:T(4,128)}, u32[]{:S(2)}, u32[]{:S(2)}) async-start(f32[128,4,1282]{2,1,0:T(4,128)} %concatenate.13), calls=%async_computation | async-start | bytes 5767168 | tf_op jit(solution)/shard_map/all_to_all | solution.py:11
  47.0 359.7 %all-gather.3.cloned.1.call-start = ((), (), s32[]{:S(2)}) async-start(), calls=%async_computation.1 | async-start | bytes 1320960 | tf_op jit(solution)/shard_map/all_gather | solution.py:46
Sparse Core Ops, SparseCore 0:
  107.9 298.7 all-gather.2
where the time goes:
time: 424 us
  waiting for transfers between devices  336 us (79%)
  matrix products  30.5 us (7%)
  local copies, waits for them, and re-layouts  27.3 us (6%)
  between operations  13.5 us (3%)
  starting transfers between devices  12.1 us (3%)
    all_gather x1, waiting for transfers between devices, on_device(): gathered = lax.all_gather(expert_out, ('seq', 'grp'), axis=0, tiled=True)  299 us
    all_to_all x1, waiting for transfers between devices, in_one_piece(): lax.all_to_all(both, axis, split_axis=split_dim, concat_axis=concat_dim,...  37.5 us
    all_to_all x1, starting transfers between devices, in_one_piece(): lax.all_to_all(both, axis, split_axis=split_dim, concat_axis=concat_dim,...  11.9 us
    concatenate x4, local copies, waits for them, and re-layouts, in_one_piece(): both = jnp.concatenate(columns, axis=along)  10.2 us
  transfers between devices with their start and end apart: 2, of which 2 were waited for; matrix products, arithmetic and copies ran while one was open for 0% of the time, Pallas kernels for 0%

commit v1 on v0

--- a/solution.py
+++ b/solution.py
@@ -43,7 +43,12 @@
     row_top = jnp.max(logits, axis=1, keepdims=True)
     row_exp = jnp.exp(logits - row_top)
     combine = (row_exp / jnp.sum(row_exp, axis=1, keepdims=True)).astype(jnp.bfloat16)
-    gathered = lax.all_gather(expert_out, ("seq", "grp"), axis=0, tiled=True)
+    gathered = jnp.concatenate(
+        lax.all_to_all(
+            jnp.stack([expert_out] * lax.axis_size(("seq", "grp"))), ("seq", "grp"), 0, 0
+        ),
+        axis=0,
+    )
     mixed = jnp.dot(combine, gathered, preferred_element_type=jnp.float32)
     return mixed.astype(jnp.bfloat16)
 

time: 424 us -> 137 us (0.32)
  waiting for transfers between devices: 336 us -> 37.7 us
  blocking collectives: 0 us -> 25.7 us
  between operations: 13.5 us -> 0.09 us
    all_gather x1 -> x0, waiting for transfers between devices: 299 us -> none  [on_device(): gathered = lax.all_gather(expert_out, ('seq', 'grp'), axis=0, tiled=True)]
    all_to_all x0 -> x1, blocking collectives: none -> 25.7 us  [on_device(): lax.all_to_all(jnp.stack([expert_out] * lax.axis_size(('seq', 'grp'))), (...]
  transfers between devices with their start and end apart: 2 -> 1, of which waited for: 2 -> 1; matrix products, arithmetic and copies ran while one was open for 0% -> 0% of each run, Pallas kernels for 0% -> 0%
where the time goes in v1:
time: 137 us; the launch traced here: 136 us
  waiting for transfers between devices  37.7 us (28%)
  matrix products  30.3 us (22%)
  local copies, waits for them, and re-layouts  26.3 us (19%)
  blocking collectives  25.7 us (19%)
  starting transfers between devices  11.9 us (9%)
  other arithmetic  4.03 us (3%)
    all_to_all x1, waiting for transfers between devices, in_one_piece(): lax.all_to_all(both, axis, split_axis=split_dim, concat_axis=concat_dim,...  37.7 us
    all_to_all x1, blocking collectives, on_device(): lax.all_to_all(jnp.stack([expert_out] * lax.axis_size(('seq', 'grp'))), (...  25.7 us
    all_to_all x1, starting transfers between devices, in_one_piece(): lax.all_to_all(both, axis, split_axis=split_dim, concat_axis=concat_dim,...  11.9 us
    concatenate x4, local copies, waits for them, and re-layouts, in_one_piece(): both = jnp.concatenate(columns, axis=along)  10.2 us
    dot_general x1, matrix products, on_device(): lax.dot_general(weights, tokens, dims, preferred_element_type=jnp.float32)  8.36 us
    dot_general x1, matrix products, on_device(): mixed = jnp.dot(combine, gathered, preferred_element_type=jnp.float32)  8.12 us
    dot_general x1, matrix products, on_device(): logits = jnp.dot(tokens, slot_keys, preferred_element_type=jnp.float32)  7.07 us
    dot_general x1, matrix products, on_device(): jnp.dot(hidden, w_out[0], preferred_element_type=jnp.float32)  6.7 us
  transfers between devices with their start and end apart: 1, of which 1 were waited for; matrix products, arithmetic and copies ran while one was open for 0% of the time, Pallas kernels for 0%

profile of v1, /device:TPU:1, one launch (start us, length us, event | category | flops | bytes accessed | tf_op | source)
XLA Modules:
  0.0 136.0 jit_solution(12681431314428755300)
XLA Ops:
  0.0 0.0 copy-start
  0.0 1.3 copy-done
  1.3 7.1 %fusion.41 = (f32[2048]{0:T(1024)S(1)}, f32[512]{0:T(512)S(1)}, f32[2048,512]{1,0:T(8,128)}) fusion(bf16[2048,1280]{1,0:T(8,128)(2,1)} %param.5, bf16[1280,512]{1,0:T(8,128)(2,1)S(1)} %copy-done), kind=kOutput, calls=%fused_computation.41 | convolution fusion | flops 2686449152 | bytes 10758144 | tf_op jit(solution)/shard_map/dot_general | solution.py:24
  8.4 0.3 concatenate.14
  8.7 0.0 copy-start.1
  8.7 8.4 %fusion.10 = f32[512,1280]{1,0:T(8,128)} fusion(bf16[2048,1280]{1,0:T(8,128)(2,1)} %param.5, f32[2048,512]{1,0:T(8,128)} %get-tuple-element.13, f32[512]{0:T(512)S(1)} %get-tuple-element.8), kind=kOutput, calls=%fused_computation.13 | convolution fusion | flops 2686451712 | bytes 12060672 | tf_op jit(solution)/shard_map/dot_general | solution.py:31
  17.1 0.0 copy-done.1
  17.1 1.6 %fusion.4 = (f32[2048]{0:T(1024)S(1)}, f32[512]{0:T(512)S(1)}) fusion(f32[2048,512]{1,0:T(8,128)S(1)} %copy-done.1, f32[2048]{0:T(1024)S(1)} %get-tuple-element.7, f32[512]{0:T(512)S(1)} %get-tuple-element.8), kind=kLoop, calls=%fused_computation.8 | loop fusion | flops 4191744 | bytes 4214784 | tf_op jit(solution)/shard_map/reduce_sum | solution.py:45
  18.7 0.3 concatenate.15
  19.0 3.9 %concatenate.10 = f32[128,4,1280]{2,1,0:T(4,128)} reshape(f32[512,1280]{1,0:T(8,128)} %fusion.10) | data formatting | bytes 5242880 | tf_op jit(solution)/shard_map/concatenate | solution.py:9
  23.0 5.6 %concatenate.13 = f32[128,4,1282]{2,1,0:T(4,128)} concatenate(f32[128,4,1280]{2,1,0:T(4,128)} %concatenate.10, f32[128,4,1]{2,1,0:T(4,128)S(1)} %concatenate.14, f32[128,4,1]{2,1,0:T(4,128)S(1)} %concatenate.15), dimensions={2} | concatenate | bytes 5251072 | tf_op jit(solution)/shard_map/concatenate | solution.py:9
  28.6 0.0 copy-start.2
  28.6 11.9 %all-to-all-start = ((f32[128,4,1282]{2,1,0:T(4,128)}), f32[128,4,1282]{2,1,0:T(4,128)}, u32[]{:S(2)}, u32[]{:S(2)}) async-start(f32[128,4,1282]{2,1,0:T(4,128)} %concatenate.13), calls=%async_computation | async-start | bytes 5767168 | tf_op jit(solution)/shard_map/all_to_all | solution.py:11
  40.5 0.0 copy-done.2
  40.5 37.7 %all-to-all-done = f32[128,4,1282]{2,1,0:T(4,128)} async-done(((f32[128,4,1282]{2,1,0:T(4,128)}), f32[128,4,1282]{2,1,0:T(4,128)}, u32[]{:S(2)}, u32[]{:S(2)}) %all-to-all-start) | async-done | bytes 2625568 | tf_op jit(solution)/shard_map/all_to_all | solution.py:11
  78.2 4.4 %all_to_all.10 = f32[512,1282]{1,0:T(8,128)} reshape(f32[128,4,1282]{2,1,0:T(4,128)} %all-to-all-done) | data formatting | bytes 5251072 | tf_op jit(solution)/shard_map/all_to_all | solution.py:11
  82.6 1.3 slice_reduce_fusion
  84.0 3.4 %slice.12 = f32[512,1280]{1,0:T(8,128)} slice(f32[512,1282]{1,0:T(8,128)} %all_to_all.10), slice={[0:512], [0:1280]} | slice | bytes 5242880 | tf_op jit(solution)/shard_map/slice | solution.py:16
  87.4 3.9 %reshape.42 = f32[128,4,1280]{2,1,0:T(4,128)} reshape(f32[512,1280]{1,0:T(8,128)} %slice.12) | data formatting | bytes 5242880 | tf_op jit(solution)/shard_map/reshape | solution.py:35
  91.3 0.1 reshape_reshape.7
  91.4 0.1 reshape_reshape.6
  91.6 2.3 %multiply_reduce_fusion = f32[4,1280]{1,0:T(4,128)S(1)} fusion(f32[128,4,1280]{2,1,0:T(4,128)} %reshape.42, f32[128,4]{1,0:T(8,128)S(1)} %get-tuple-element.12), kind=kLoop, calls=%fused_computation.11 | loop fusion | flops 1305600 | bytes 2643968 | tf_op jit(solution)/shard_map/reduce_sum | solution.py:35
  93.9 6.7 %fusion.7 = bf16[4,1280]{1,0:T(4,128)(2,1)S(1)} fusion(bf16[1,2560,1280]{2,1,0:T(8,128)(2,1)} %param.9, bf16[1,1280,2560]{2,1,0:T(8,128)(2,1)} %param.8, f32[4,1280]{1,0:T(4,128)S(1)} %multiply_reduce_fusion, f32[1280]{0:T(1024)S(1)} %reduce.2, f32[4]{0:T(128)S(1)} %get-tuple-element.11), kind=kOutput, calls=%fused_computation.12 | convolution fusion | flops 52541440 | bytes 13143056 | tf_op jit(solution)/shard_map/dot_general | solution.py:42
  100.6 0.3 stack.2
  101.0 25.7 %all_to_all.14 = bf16[128,4,1280]{2,1,0:T(4,128)(2,1)S(1)} all-to-all(bf16[128,4,1280]{2,1,0:T(4,128)(2,1)S(1)} %stack.2), channel_id=1, replica_groups=mesh['seq'=16,'grp'=8] {'seq','grp'}, dimensions={0} | all-to-all | bytes 2621440 | tf_op jit(solution)/shard_map/all_to_all | solution.py:47
  126.7 1.2 reshape.43
  127.9 8.1 %convolution_convert_fusion = bf16[2048,1280]{1,0:T(8,128)(2,1)} fusion(bf16[512,1280]{1,0:T(8,128)(2,1)} %reshape.43, f32[2048,512]{1,0:T(8,128)} %get-tuple-element.13, f32[2048]{0:T(1024)S(1)} %get-tuple-element.5, f32[2048]{0:T(1024)S(1)} %get-tuple-element.7), kind=kOutput, calls=%fused_computation | convolution fusion | flops 2690121728 | bytes 10764288 | tf_op jit(solution)/shard_map/dot_general | solution.py:52
  (3 shorter events, 0.1 us)
Async XLA Ops:
  0.0 1.3 copy-start
  8.7 8.4 %copy-start.1 = (f32[2048,512]{1,0:T(8,128)S(1)}, f32[2048,512]{1,0:T(8,128)}, u32[]{:S(2)}) copy-start(f32[2048,512]{1,0:T(8,128)} %get-tuple-element.13) | copy-start | bytes 12582916
  28.6 11.9 %copy-start.2 = (f32[1,1280]{1,0:T(1,128)S(1)}, f32[1,1280]{1,0:T(1,128)}, u32[]{:S(2)}) copy-start(f32[1,1280]{1,0:T(1,128)} %param.7) | copy-start | bytes 15364
  28.6 49.6 %all-to-all-start = ((f32[128,4,1282]{2,1,0:T(4,128)}), f32[128,4,1282]{2,1,0:T(4,128)}, u32[]{:S(2)}, u32[]{:S(2)}) async-start(f32[128,4,1282]{2,1,0:T(4,128)} %concatenate.13), calls=%async_computation | async-start | bytes 5767168 | tf_op jit(solution)/shard_map/all_to_all | solution.py:11
